TPU v7x, 256 devices: a whole 4x4x8 slice. The times are simulated.
256 devices in a mesh: dp: 16 (over y, z_lo, core), own: 16 (over x, z_hi).
Axes of the slice: x: 4, y: 4, z: 8 (z_hi: 4, z_lo: 2; z = z_hi * 2 + z_lo), core: 2. Of those that a mesh axis runs over, the one named last changes fastest.
Arguments:
- grads: bfloat16 [16, 32, 768, 768], P('dp', 'own'), may hold values from -0.059814453 to 0.059814453
- owner: int32 [32], replicated, may hold values from 0 to 15, as said below
- weights: float32 [64, 768, 768], P('own', 'dp'), may hold values from -6 to 6
- stat_left: float32 [64, 768, 768], P('own', 'dp'), may hold values from -3 to 3
- stat_right: float32 [64, 768, 768], P('own', 'dp'), may hold values from -3 to 3
- adam_second: float32 [64, 768, 768], P('own', 'dp'), may hold values from 0.0002 to 1
- root_left: bfloat16 [64, 768, 768], P('own', 'dp'), may hold values from -0.21875 to 0.21875
- root_right: bfloat16 [64, 768, 768], P('own', 'dp'), may hold values from -0.21875 to 0.21875
Outputs:
- new_weights: bfloat16 [64, 768, 768], P('own')
- new_left: float32 [64, 768, 768], P('own', 'dp')
- new_right: float32 [64, 768, 768], P('own', 'dp')
- new_second: float32 [64, 768, 768], P('own', 'dp')
Inputs may be any that keep to these rules, and one draw needn't show every extreme that they name: The 2 blocks 2 * j to 2 * j + 1 have different owners, for every j; one owner holds exactly 4 blocks and none holds more.
All inputs are finite; a program needn't handle non-finite values.
Results may differ from a plain program's by a relative error of at most 0.0095.
Values may be sent and summed in bfloat16 or wider, within the bound.
No kernel may reach another device: no remote copies, remote signals or barrier semaphores. Data moves between devices by JAX's collectives and lax.ppermute only.
A program may use at most 64 MiB of HBM per device.

v0:
```python
import jax
import jax.numpy as jnp
from jax import lax
from jax.sharding import PartitionSpec as P


def slot_index(owner, capacity):
    count = owner.shape[0]
    same = owner[:, None] == owner[None, :]
    earlier = (
        jnp.arange(count, dtype=jnp.int32)[None, :] < jnp.arange(count, dtype=jnp.int32)[:, None]
    )
    rank = jnp.sum((same & earlier).astype(jnp.int32), axis=1)
    return owner * capacity + rank


def on_device(grads, owner, weights, stat_left, stat_right, adam_second, root_left, root_right):
    per_index = grads.shape[1]
    width = grads.shape[3]
    capacity = 2 * per_index
    replicas = lax.axis_size("dp")
    me = lax.axis_index("own")
    rep = lax.axis_index("dp")
    col_count = width // replicas
    summed = lax.psum_scatter(
        grads[0].astype(jnp.float32).astype(jnp.bfloat16), "dp", scatter_dimension=1, tiled=True
    )
    row_count = summed.shape[1]
    slot = slot_index(owner, capacity)
    targets = me * capacity + jnp.arange(capacity, dtype=jnp.int32)
    every = lax.all_gather(summed, "own", axis=0, tiled=True)
    pick = (slot[None, :] == targets[:, None]).astype(jnp.bfloat16)
    mine = jnp.dot(
        pick, every.reshape(every.shape[0], row_count * width), preferred_element_type=jnp.float32
    )
    mine = mine.astype(jnp.bfloat16).reshape(capacity, row_count, width)
    full = lax.all_gather(mine, "dp", axis=1, tiled=True)
    new_left = 0.5 * stat_left + 0.5 * jnp.einsum(
        "srd,sbd->srb", mine, full, preferred_element_type=jnp.float32
    )
    columns = lax.dynamic_slice_in_dim(full, rep * col_count, col_count, 2)
    new_right = 0.5 * stat_right + 0.5 * jnp.einsum(
        "sbc,sbd->scd", columns, full, preferred_element_type=jnp.float32
    )
    grad32 = mine.astype(jnp.float32)
    new_second = 0.9 * adam_second + 0.1 * grad32 * grad32
    adam_dir = grad32 / (jnp.sqrt(new_second) + 1e-08)
    half = jnp.einsum("srb,sbd->srd", root_left, full, preferred_element_type=jnp.float32).astype(
        jnp.bfloat16
    )
    precond = jnp.einsum(
        "src,scd->srd",
        half,
        lax.all_gather(root_right, "dp", axis=1, tiled=True),
        preferred_element_type=jnp.float32,
    )
    adam_sq = jnp.sum(adam_dir * adam_dir, axis=(1, 2))
    prec_sq = jnp.sum(precond * precond, axis=(1, 2))
    adam_total, prec_total = lax.psum((adam_sq, prec_sq), "dp")
    graft = jnp.sqrt(adam_total) / (jnp.sqrt(prec_total) + 1e-06)
    fresh_rows = (weights - graft[:, None, None] * precond).astype(jnp.bfloat16)
    new_weights = lax.all_gather(fresh_rows, "dp", axis=1, tiled=True)
    return (new_weights, new_left, new_right, new_second)


def solution(mesh):
    placed = (
        P("dp", "own", None, None),
        P(),
        P("own", "dp", None),
        P("own", "dp", None),
        P("own", "dp", None),
        P("own", "dp", None),
        P("own", "dp", None),
        P("own", "dp", None),
    )
    return jax.shard_map(
        on_device,
        mesh=mesh,
        in_specs=placed,
        out_specs=(
            P("own", None, None),
            P("own", "dp", None),
            P("own", "dp", None),
            P("own", "dp", None),
        ),
        check_vma=False,
    )
```

profile of v0, /device:TPU:1, one launch (start us, length us, event | category | flops | bytes accessed | tf_op | source)
XLA Modules:
  0.0 314.4 jit_solution(17411451454313605039)
XLA Ops:
  7.2 0.0 copy-start
  7.2 0.0 reduce-scatter.2.cloned.1.call-start
  7.2 0.7 reduce-scatter.2.cloned.1.call-update
  7.9 0.0 copy-start.3
  7.9 0.0 all-gather.5.cloned.1.call-start
  8.0 71.1 %reduce-scatter.2.cloned.1.call-done = bf16[2,48,768]{2,1,0:T(8,128)(2,1)} async-done(((bf16[2,768,768]{2,1,0:T(8,128)(2,1)}), bf16[2,48,768]{2,1,0:T(8,128)(2,1)}) %reduce-scatter.2.cloned.1.call-update) | async-done | bytes 147472 | tf_op jit(solution)/shard_map/reduce_scatter | solution.py:25
  79.1 0.0 all-gather.5.cloned.1.call-update
  79.1 0.0 all-gather.9.cloned.1.call-start
  79.1 0.7 all-gather.9.cloned.1.call-update
  79.8 0.0 all-gather.7.cloned.1.call-start
  79.9 0.9 convert_reduce_fusion
  80.8 0.7 multiply_add_fusion
  81.5 62.1 %all-gather.5.cloned.1.call-done = bf16[32,48,768]{2,1,0:T(8,128)(2,1)} async-done(((bf16[2,48,768]{2,1,0:T(8,128)(2,1)}), bf16[32,48,768]{2,1,0:T(8,128)(2,1)}) %all-gather.5.cloned.1.call-update) | async-done | bytes 2359312 | tf_op jit(solution)/shard_map/all_gather | solution.py:31
  143.5 2.4 copy.16
  146.0 0.5 convolution_convert_fusion
  146.5 0.7 copy.25
  147.2 0.0 all-gather.7.cloned.1.call-update
  147.2 0.0 all-gather.11.cloned.1.call-start
  147.3 0.0 copy-done.3
  147.3 1.1 fusion.6
  148.4 0.0 copy-start.4
  148.4 0.0 copy-start.1
  148.4 36.5 %all-gather.9.cloned.1.call-done = bf16[4,768,768]{2,1,0:T(8,128)(2,1)} async-done(((bf16[4,48,768]{2,1,0:T(8,128)(2,1)}), bf16[4,768,768]{2,1,0:T(8,128)(2,1)}) %all-gather.9.cloned.1.call-update) | async-done | bytes 4718608 | tf_op jit(solution)/shard_map/all_gather | solution.py:54
  185.0 43.2 %all-gather.7.cloned.1.call-done = bf16[4,768,768]{2,1,0:T(8,128)(2,1)} async-done(((bf16[4,48,768]{2,1,0:T(8,128)(2,1)}), bf16[4,768,768]{2,1,0:T(8,128)(2,1)}) %all-gather.7.cloned.1.call-update) | async-done | bytes 4718608 | tf_op jit(solution)/shard_map/all_gather | solution.py:37
  228.2 0.0 copy-done
  228.2 5.6 %multiply_reduce_fusion = (f32[4]{0:T(128)S(1)}, f32[4,48,768]{2,1,0:T(8,128)S(1)}) fusion(bf16[4,768,768]{2,1,0:T(8,128)(2,1)} %all-gather.9.cloned.1.call-done, bf16[4,48,768]{2,1,0:T(8,128)(2,1)S(1)} %copy-done, bf16[4,768,768]{2,1,0:T(8,128)(2,1)} %all-gather.7.cloned.1.call-done), kind=kOutput, calls=%fused_computation.13 | convolution fusion | flops 453427200 | bytes 10321936 | tf_op jit(solution)/shard_map/src,scd->srd/dot_general | solution.py:51
  233.8 26.8 %all-reduce = (f32[4]{0:T(128)S(1)}, f32[4]{0:T(128)S(1)}) all-reduce(f32[4]{0:T(128)S(1)} %get-tuple-element.8, f32[4]{0:T(128)S(1)} %get-tuple-element.6), channel_id=1, replica_groups=mesh['dp'=16,'own'=16] {'dp'}, use_global_device_ids=true, to_apply=%region_5.0 | all-reduce | flops 8 | bytes 64 | tf_op jit(solution)/shard_map/psum | solution.py:59
  260.5 0.0 copy-done.4
  260.5 0.8 subtract_convert_fusion
  261.4 0.0 slice-start
  261.4 0.0 copy-start.2
  261.4 0.0 all-gather.11.cloned.1.call-update
  261.4 0.0 copy-done.1
  261.4 0.0 slice-start.1
  261.4 5.0 %fusion.1 = f32[4,48,768]{2,1,0:T(8,128)} fusion(f32[4,48,768]{2,1,0:T(8,128)S(1)} %copy-done.1, bf16[4,768,768]{2,1,0:T(8,128)(2,1)} %all-gather.7.cloned.1.call-done, s32[]{:T(128)S(6)} %select_n.3), kind=kOutput, calls=%fused_computation.4 | convolution fusion | flops 226787328 | bytes 6684676 | tf_op jit(solution)/shard_map/sbc,sbd->scd/dot_general | solution.py:42
  266.4 0.0 slice-done
  266.4 0.0 copy-done.2
  266.4 0.0 slice-done.1
  266.4 2.3 fusion
  268.7 34.3 %all-gather.11.cloned.1.call-done = bf16[4,768,768]{2,1,0:T(8,128)(2,1)} async-done(((bf16[4,48,768]{2,1,0:T(8,128)(2,1)}), bf16[4,768,768]{2,1,0:T(8,128)(2,1)}) %all-gather.11.cloned.1.call-update) | async-done | bytes 4718608 | tf_op jit(solution)/shard_map/all_gather | solution.py:62
  303.1 4.8 %copy.27 = bf16[4,768,768]{2,1,0:T(8,128)(2,1)} copy(bf16[4,768,768]{2,1,0:T(8,128)(2,1)} %all-gather.11.cloned.1.call-done) | data formatting | bytes 9437184
  (3 shorter events, 0.0 us)
Async XLA Ops:
  7.2 221.0 %copy-start = (bf16[4,48,768]{2,1,0:T(8,128)(2,1)S(1)}, bf16[4,48,768]{2,1,0:T(8,128)(2,1)}, u32[]{:S(2)}) copy-start(bf16[4,48,768]{2,1,0:T(8,128)(2,1)} %param.14) | copy-start | bytes 884740
  7.2 71.9 %reduce-scatter.2.cloned.1.call-start = ((), (), s32[]{:S(2)}) async-start(), calls=%async_computation.1 | async-start | bytes 2506752 | tf_op jit(solution)/shard_map/reduce_scatter | solution.py:25
  7.9 139.4 %copy-start.3 = (f32[4,48,768]{2,1,0:T(8,128)S(1)}, f32[4,48,768]{2,1,0:T(8,128)}, u32[]{:S(2)}) copy-start(f32[4,48,768]{2,1,0:T(8,128)} %param.13) | copy-start | bytes 1769476
  7.9 135.6 %all-gather.5.cloned.1.call-start = ((), (), s32[]{:S(2)}) async-start(), calls=%async_computation.2 | async-start | bytes 2506752 | tf_op jit(solution)/shard_map/all_gather | solution.py:31
  79.1 105.9 %all-gather.9.cloned.1.call-start = ((), (), s32[]{:S(2)}) async-start(), calls=%async_computation.4 | async-start | bytes 5013504 | tf_op jit(solution)/shard_map/all_gather | solution.py:54
  79.8 148.3 %all-gather.7.cloned.1.call-start = ((), (), s32[]{:S(2)}) async-start(), calls=%async_computation.3 | async-start | bytes 5013504 | tf_op jit(solution)/shard_map/all_gather | solution.py:37
  147.2 155.8 %all-gather.11.cloned.1.call-start = ((), (), s32[]{:S(2)}) async-start(), calls=%async_computation.5 | async-start | bytes 5013504 | tf_op jit(solution)/shard_map/all_gather | solution.py:62
  148.4 112.1 %copy-start.4 = (f32[4,48,768]{2,1,0:T(8,128)S(1)}, f32[4,48,768]{2,1,0:T(8,128)}, u32[]{:S(2)}) copy-start(f32[4,48,768]{2,1,0:T(8,128)} %param.10) | copy-start | bytes 1769476
  148.4 113.0 %copy-start.1 = (f32[4,48,768]{2,1,0:T(8,128)S(1)}, f32[4,48,768]{2,1,0:T(8,128)}, u32[]{:S(2)}) copy-start(f32[4,48,768]{2,1,0:T(8,128)} %param.12) | copy-start | bytes 1769476
  261.4 5.0 %slice-start = ((s8[4718592]{0:T(1024)(128)(4,1)}), s8[524288]{0:T(1024)(128)(4,1)S(1)}, s32[]{:S(2)}) async-start(s8[4718592]{0:T(1024)(128)(4,1)} %bitcast.19), calls=%async_computation.6 | async-start | bytes 1048576
  261.4 5.0 %copy-start.2 = (f32[4,48,768]{2,1,0:T(8,128)S(1)}, f32[4,48,768]{2,1,0:T(8,128)}, u32[]{:S(2)}) copy-start(f32[4,48,768]{2,1,0:T(8,128)} %param.11) | copy-start | bytes 1769476
  261.4 5.0 %slice-start.1 = ((s8[4718592]{0:T(1024)(128)(4,1)}), s8[4194304]{0:T(1024)(128)(4,1)S(1)}, s32[]{:S(2)}) async-start(s8[4718592]{0:T(1024)(128)(4,1)} %bitcast.19), calls=%async_computation.7 | async-start | bytes 8388608
Sparse Core Ops, SparseCore 0:
  10.6 68.4 reduce-scatter.1
  81.5 61.9 all-gather.4
  145.3 39.5 all-gather.8
  187.2 40.9 all-gather.6
  261.5 41.4 all-gather.10
where the time goes:
time: 315 us; the launch traced here: 314 us
  waiting for transfers between devices  249 us (79%)
  blocking collectives  26.8 us (9%)
  between operations  13.9 us (4%)
  matrix products  13.4 us (4%)
  local copies, waits for them, and re-layouts  8.03 us (3%)
  other arithmetic  3.58 us (1%)
    reduce_scatter x1, waiting for transfers between devices, on_device(): lax.psum_scatter(grads[0].astype(jnp.float32).astype(jnp.bfloat16), 'dp',...  71.1 us
    all_gather x1, waiting for transfers between devices, on_device(): every = lax.all_gather(summed, 'own', axis=0, tiled=True)  62.1 us
    all_gather x1, waiting for transfers between devices, on_device(): full = lax.all_gather(mine, 'dp', axis=1, tiled=True)  43.2 us
    all_gather x1, waiting for transfers between devices, on_device(): lax.all_gather(root_right, 'dp', axis=1, tiled=True)  36.5 us
    all_gather x1, waiting for transfers between devices, on_device(): new_weights = lax.all_gather(fresh_rows, 'dp', axis=1, tiled=True)  34.3 us
    psum x1, blocking collectives, on_device(): adam_total, prec_total = lax.psum((adam_sq, prec_sq), 'dp')  26.8 us
    unnamed x17, local copies, waits for them, and re-layouts  8.03 us
  transfers between devices with their start and end apart: 5, of which 5 were waited for; matrix products, arithmetic and copies ran while one was open for 4% of the time, Pallas kernels for 0%

commit v1 on v0

--- a/solution.py
+++ b/solution.py
@@ -51,7 +51,9 @@
     precond = jnp.einsum(
         "src,scd->srd",
         half,
-        lax.all_gather(root_right, "dp", axis=1, tiled=True),
+        jnp.concatenate(
+            lax.all_to_all(jnp.stack([root_right] * lax.axis_size("dp")), "dp", 0, 0), axis=1
+        ),
         preferred_element_type=jnp.float32,
     )
     adam_sq = jnp.sum(adam_dir * adam_dir, axis=(1, 2))

time: 315 us -> 284 us (0.902)
  waiting for transfers between devices: 249 us -> 203 us
  local copies, waits for them, and re-layouts: 8.03 us -> 16.7 us
  starting transfers between devices: 0.19 us -> 8.2 us
    all_gather x1 -> x0, waiting for transfers between devices: 36.5 us -> none  [on_device(): lax.all_gather(root_right, 'dp', axis=1, tiled=True)]
    all_gather x1, waiting for transfers between devices: 43.2 us -> 21.1 us  [on_device(): full = lax.all_gather(mine, 'dp', axis=1, tiled=True)]
    all_to_all x0 -> x1, waiting for transfers between devices: none -> 11.9 us  [on_device(): lax.all_to_all(jnp.stack([root_right] * lax.axis_size('dp')), 'dp', 0, 0)]
    all_to_all x0 -> x1, starting transfers between devices: none -> 8.04 us  [on_device(): lax.all_to_all(jnp.stack([root_right] * lax.axis_size('dp')), 'dp', 0, 0)]
    reshape x0 -> x1, local copies, waits for them, and re-layouts: none -> 5.05 us  [on_device(): jnp.concatenate(lax.all_to_all(jnp.stack([root_right] * lax.axis_size('dp...]
    another operation x0 -> x1, local copies, waits for them, and re-layouts: none -> 3.61 us  [on_device(): jnp.stack([root_right] * lax.axis_size('dp'))]
    unnamed x17 -> x19, local copies, waits for them, and re-layouts: 8.03 us -> 8.04 us
  transfers between devices with their start and end apart: 5 -> 5, of which waited for: 5 -> 5; matrix products, arithmetic and copies ran while one was open for 4% -> 7% of each run, Pallas kernels for 0% -> 0%
where the time goes in v1:
time: 284 us
  waiting for transfers between devices  203 us (71%)
  blocking collectives  26.8 us (9%)
  local copies, waits for them, and re-layouts  16.7 us (6%)
  between operations  13.8 us (5%)
  matrix products  13.4 us (5%)
  starting transfers between devices  8.2 us (3%)
    reduce_scatter x1, waiting for transfers between devices, on_device(): lax.psum_scatter(grads[0].astype(jnp.float32).astype(jnp.bfloat16), 'dp',...  71.1 us
    all_gather x1, waiting for transfers between devices, on_device(): every = lax.all_gather(summed, 'own', axis=0, tiled=True)  63.4 us
    all_gather x1, waiting for transfers between devices, on_device(): new_weights = lax.all_gather(fresh_rows, 'dp', axis=1, tiled=True)  34.3 us
    psum x1, blocking collectives, on_device(): adam_total, prec_total = lax.psum((adam_sq, prec_sq), 'dp')  26.8 us
    all_gather x1, waiting for transfers between devices, on_device(): full = lax.all_gather(mine, 'dp', axis=1, tiled=True)  21.1 us
    all_to_all x1, waiting for transfers between devices, on_device(): lax.all_to_all(jnp.stack([root_right] * lax.axis_size('dp')), 'dp', 0, 0)  11.9 us
    all_to_all x1, starting transfers between devices, on_device(): lax.all_to_all(jnp.stack([root_right] * lax.axis_size('dp')), 'dp', 0, 0)  8.04 us
    unnamed x19, local copies, waits for them, and re-layouts  8.04 us
  transfers between devices with their start and end apart: 5, of which 5 were waited for; matrix products, arithmetic and copies ran while one was open for 7% of the time, Pallas kernels for 0%

profile of v1, /device:TPU:1, one launch (start us, length us, event | category | flops | bytes accessed | tf_op | source)
XLA Modules:
  0.0 283.7 jit_solution(17649928235604727082)
XLA Ops:
  7.2 0.0 copy-start
  7.2 0.0 reduce-scatter.2.cloned.1.call-start
  7.2 0.7 reduce-scatter.2.cloned.1.call-update
  7.9 0.0 all-gather.4.cloned.1.call-start
  8.0 71.1 %reduce-scatter.2.cloned.1.call-done = bf16[2,48,768]{2,1,0:T(8,128)(2,1)} async-done(((bf16[2,768,768]{2,1,0:T(8,128)(2,1)}), bf16[2,48,768]{2,1,0:T(8,128)(2,1)}) %reduce-scatter.2.cloned.1.call-update) | async-done | bytes 147472 | tf_op jit(solution)/shard_map/reduce_scatter | solution.py:25
  79.1 0.0 all-gather.4.cloned.1.call-update
  79.1 3.6 %stack.2 = bf16[16,4,48,768]{3,2,1,0:T(8,128)(2,1)} broadcast(bf16[4,48,768]{2,1,0:T(8,128)(2,1)} %param.15), dimensions={1,2,3} | broadcast | bytes 5013504 | tf_op jit(solution)/shard_map/stack | solution.py:55
  82.7 0.0 copy-start.5
  82.7 8.0 %all-to-all-start = ((bf16[16,4,48,768]{3,2,1,0:T(8,128)(2,1)}), bf16[16,4,48,768]{3,2,1,0:T(8,128)(2,1)}, u32[]{:S(2)}, u32[]{:S(2)}) async-start(bf16[16,4,48,768]{3,2,1,0:T(8,128)(2,1)} %stack.2), calls=%async_computation.1 | async-start | bytes 9437184 | tf_op jit(solution)/shard_map/all_to_all | solution.py:55
  90.7 0.0 all-gather.6.cloned.1.call-start
  90.8 0.0 copy-done.5
  90.8 0.2 convert_reduce_fusion
  91.0 63.4 %all-gather.4.cloned.1.call-done = bf16[32,48,768]{2,1,0:T(8,128)(2,1)} async-done(((bf16[2,48,768]{2,1,0:T(8,128)(2,1)}), bf16[32,48,768]{2,1,0:T(8,128)(2,1)}) %all-gather.4.cloned.1.call-update) | async-done | bytes 2359312 | tf_op jit(solution)/shard_map/all_gather | solution.py:31
  154.4 2.4 copy.18
  156.8 0.5 convolution_convert_fusion
  157.3 0.7 copy.27
  158.1 0.0 all-gather.6.cloned.1.call-update
  158.1 0.0 all-gather.8.cloned.1.call-start
  158.1 11.9 %all-to-all-done = bf16[16,4,48,768]{3,2,1,0:T(8,128)(2,1)} async-done(((bf16[16,4,48,768]{3,2,1,0:T(8,128)(2,1)}), bf16[16,4,48,768]{3,2,1,0:T(8,128)(2,1)}, u32[]{:S(2)}, u32[]{:S(2)}) %all-to-all-start) | async-done | bytes 4718624 | tf_op jit(solution)/shard_map/all_to_all | solution.py:55
  170.1 0.0 copy-start.3
  170.1 5.1 %copy.15 = bf16[4,16,48,768]{3,2,1,0:T(8,128)(2,1)} copy(bf16[4,16,48,768]{3,2,0,1:T(8,128)(2,1)} %bitcast.1) | data formatting | bytes 9437184 | tf_op jit(solution)/shard_map/reshape | solution.py:54
  175.1 0.0 copy-done.3
  175.1 1.1 fusion.6
  176.3 21.1 %all-gather.6.cloned.1.call-done = bf16[4,768,768]{2,1,0:T(8,128)(2,1)} async-done(((bf16[4,48,768]{2,1,0:T(8,128)(2,1)}), bf16[4,768,768]{2,1,0:T(8,128)(2,1)}) %all-gather.6.cloned.1.call-update) | async-done | bytes 4718608 | tf_op jit(solution)/shard_map/all_gather | solution.py:37
  197.4 0.0 copy-done
  197.4 0.0 copy-start.4
  197.4 0.0 copy-start.1
  197.4 5.7 %multiply_reduce_fusion = (f32[4]{0:T(128)S(1)}, f32[4,48,768]{2,1,0:T(8,128)S(1)}) fusion(bf16[4,768,768]{2,1,0:T(8,128)(2,1)} %bitcast.23, bf16[4,48,768]{2,1,0:T(8,128)(2,1)S(1)} %copy-done, bf16[4,768,768]{2,1,0:T(8,128)(2,1)} %all-gather.6.cloned.1.call-done), kind=kOutput, calls=%fused_computation.13 | convolution fusion | flops 453427200 | bytes 10321936 | tf_op jit(solution)/shard_map/src,scd->srd/dot_general | solution.py:51
  203.1 26.8 %all-reduce = (f32[4]{0:T(128)S(1)}, f32[4]{0:T(128)S(1)}) all-reduce(f32[4]{0:T(128)S(1)} %get-tuple-element.8, f32[4]{0:T(128)S(1)} %get-tuple-element.6), channel_id=1, replica_groups=mesh['dp'=16,'own'=16] {'dp'}, use_global_device_ids=true, to_apply=%region_5.0 | all-reduce | flops 8 | bytes 64 | tf_op jit(solution)/shard_map/psum | solution.py:61
  229.9 0.0 copy-done.4
  229.9 0.8 subtract_convert_fusion
  230.7 0.0 slice-start
  230.7 0.0 copy-start.2
  230.7 0.0 all-gather.8.cloned.1.call-update
  230.7 0.0 copy-done.1
  230.8 0.0 slice-start.1
  230.8 5.0 %fusion.1 = f32[4,48,768]{2,1,0:T(8,128)} fusion(f32[4,48,768]{2,1,0:T(8,128)S(1)} %copy-done.1, bf16[4,768,768]{2,1,0:T(8,128)(2,1)} %all-gather.6.cloned.1.call-done, s32[]{:T(128)S(6)} %select_n.3), kind=kOutput, calls=%fused_computation.4 | convolution fusion | flops 226787328 | bytes 6684676 | tf_op jit(solution)/shard_map/sbc,sbd->scd/dot_general | solution.py:42
  235.7 0.0 slice-done
  235.7 0.0 copy-done.2
  235.7 0.0 slice-done.1
  235.8 2.3 fusion
  238.1 34.3 %all-gather.8.cloned.1.call-done = bf16[4,768,768]{2,1,0:T(8,128)(2,1)} async-done(((bf16[4,48,768]{2,1,0:T(8,128)(2,1)}), bf16[4,768,768]{2,1,0:T(8,128)(2,1)}) %all-gather.8.cloned.1.call-update) | async-done | bytes 4718608 | tf_op jit(solution)/shard_map/all_gather | solution.py:64
  272.3 4.8 %copy.29 = bf16[4,768,768]{2,1,0:T(8,128)(2,1)} copy(bf16[4,768,768]{2,1,0:T(8,128)(2,1)} %all-gather.8.cloned.1.call-done) | data formatting | bytes 9437184
  (4 shorter events, 0.0 us)
Async XLA Ops:
  7.2 190.2 %copy-start = (bf16[4,48,768]{2,1,0:T(8,128)(2,1)S(1)}, bf16[4,48,768]{2,1,0:T(8,128)(2,1)}, u32[]{:S(2)}) copy-start(bf16[4,48,768]{2,1,0:T(8,128)(2,1)} %param.14) | copy-start | bytes 884740
  7.2 71.9 %reduce-scatter.2.cloned.1.call-start = ((), (), s32[]{:S(2)}) async-start(), calls=%async_computation.2 | async-start | bytes 2506752 | tf_op jit(solution)/shard_map/reduce_scatter | solution.py:25
  7.9 146.5 %all-gather.4.cloned.1.call-start = ((), (), s32[]{:S(2)}) async-start(), calls=%async_computation.3 | async-start | bytes 2506752 | tf_op jit(solution)/shard_map/all_gather | solution.py:31
  82.7 8.1 %copy-start.5 = (s32[32]{0:T(128)S(1)}, s32[32]{0:T(128)}, u32[]{:S(2)}) copy-start(s32[32]{0:T(128)} %param.9) | copy-start | bytes 388
  82.7 87.4 %all-to-all-start = ((bf16[16,4,48,768]{3,2,1,0:T(8,128)(2,1)}), bf16[16,4,48,768]{3,2,1,0:T(8,128)(2,1)}, u32[]{:S(2)}, u32[]{:S(2)}) async-start(bf16[16,4,48,768]{3,2,1,0:T(8,128)(2,1)} %stack.2), calls=%async_computation.1 | async-start | bytes 9437184 | tf_op jit(solution)/shard_map/all_to_all | solution.py:55
  90.7 106.6 %all-gather.6.cloned.1.call-start = ((), (), s32[]{:S(2)}) async-start(), calls=%async_computation.4 | async-start | bytes 5013504 | tf_op jit(solution)/shard_map/all_gather | solution.py:37
  158.1 114.2 %all-gather.8.cloned.1.call-start = ((), (), s32[]{:S(2)}) async-start(), calls=%async_computation.5 | async-start | bytes 5013504 | tf_op jit(solution)/shard_map/all_gather | solution.py:64
  170.1 5.1 %copy-start.3 = (f32[4,48,768]{2,1,0:T(8,128)S(1)}, f32[4,48,768]{2,1,0:T(8,128)}, u32[]{:S(2)}) copy-start(f32[4,48,768]{2,1,0:T(8,128)} %param.13) | copy-start | bytes 1769476
  197.4 32.5 %copy-start.4 = (f32[4,48,768]{2,1,0:T(8,128)S(1)}, f32[4,48,768]{2,1,0:T(8,128)}, u32[]{:S(2)}) copy-start(f32[4,48,768]{2,1,0:T(8,128)} %param.10) | copy-start | bytes 1769476
  197.4 33.4 %copy-start.1 = (f32[4,48,768]{2,1,0:T(8,128)S(1)}, f32[4,48,768]{2,1,0:T(8,128)}, u32[]{:S(2)}) copy-start(f32[4,48,768]{2,1,0:T(8,128)} %param.12) | copy-start | bytes 1769476
  230.7 5.0 %slice-start = ((s8[4718592]{0:T(1024)(128)(4,1)}), s8[524288]{0:T(1024)(128)(4,1)S(1)}, s32[]{:S(2)}) async-start(s8[4718592]{0:T(1024)(128)(4,1)} %bitcast.21), calls=%async_computation.6 | async-start | bytes 1048576
  230.7 5.0 %copy-start.2 = (f32[4,48,768]{2,1,0:T(8,128)S(1)}, f32[4,48,768]{2,1,0:T(8,128)}, u32[]{:S(2)}) copy-start(f32[4,48,768]{2,1,0:T(8,128)} %param.11) | copy-start | bytes 1769476
  230.8 5.0 %slice-start.1 = ((s8[4718592]{0:T(1024)(128)(4,1)}), s8[4194304]{0:T(1024)(128)(4,1)S(1)}, s32[]{:S(2)}) async-start(s8[4718592]{0:T(1024)(128)(4,1)} %bitcast.21), calls=%async_computation.7 | async-start | bytes 8388608
Sparse Core Ops, SparseCore 0:
  10.6 68.4 reduce-scatter.1
  81.5 72.8 all-gather.3
  158.2 39.1 all-gather.5
  230.9 41.4 all-gather.7
